TPU v7x, 512 devices: a whole 4x8x8 slice. The times are simulated.
512 devices in a mesh: dp: 32 (over x, y_hi, core), fsdp: 16 (over y_lo, z).
Axes of the slice: x: 4, y: 8 (y_hi: 4, y_lo: 2; y = y_hi * 2 + y_lo), z: 8, core: 2. Of those that a mesh axis runs over, the one named last changes fastest.
Arguments:
- hidden: bfloat16 [4, 2048, 16, 4096], P(None, 'dp', 'fsdp'), may hold values from -6 to 6
- frozen_query_rows: bfloat16 [4, 2048, 16, 2048], P(None, 'dp', 'fsdp'), may hold values from -10 to 10
- output_gradient: bfloat16 [4, 2048, 16, 2048], P(None, 'dp', 'fsdp'), may hold values from -6 to 6
- token_log_ratio: float32 [4, 2048, 16], P(None, 'dp', 'fsdp'), may hold values from -0.15625 to 0.15625
- lengths: int32 [4], replicated, may hold values from 1 to 32768, as said below
- response_win_probability: float32 [4], replicated, may hold values from 0.05 to 0.95
- cached_prompt_keys: bfloat16 [1024, 512], P('fsdp'), may hold values from -7.5 to 7.5
- cached_prompt_values: bfloat16 [1024, 512], P('fsdp'), may hold values from -6 to 6
- adapter_down_factor: bfloat16 [4096, 64], P('fsdp'), may hold values from -0.09375 to 0.09375
- adapter_up_factor: bfloat16 [64, 2048], P(None, 'fsdp'), may hold values from -0.125 to 0.125
- attention_norm_gain: bfloat16 [4096], P('fsdp'), may hold values from 0.5 to 1.5
Outputs:
- grad_down: float32 [4096, 64], P('fsdp')
- grad_up: float32 [64, 2048], P(None, 'fsdp')
- seq_ratio: float32 [4], replicated
Inputs may be any that keep to these rules, and one draw needn't show every extreme that they name: The lengths sum to 65472 and the longest is exactly 32768.
All inputs are finite; a program needn't handle non-finite values.
Results may differ from a plain program's by a relative error of at most 0.012.
Values may be sent and summed in bfloat16 or wider, within the bound.
A program may use at most 128 MiB of HBM per device.

v0:
```python
import math
import jax
import jax.numpy as jnp
from jax import lax
from jax.sharding import PartitionSpec as P

HEAD_SIZE = 128
QUERY_HEADS = 16
KEY_VALUE_HEADS = 4
target_scale = 1.0
norm_epsilon = 1e-05


def attend(query_vectors, cotangent, key_rows, value_rows):
    row_count = query_vectors.shape[0]
    queries_per_group = QUERY_HEADS // KEY_VALUE_HEADS
    score_scale = 1.0 / math.sqrt(HEAD_SIZE)
    pieces = []
    for shared_key_head in range(KEY_VALUE_HEADS):
        head_start = shared_key_head * queries_per_group * HEAD_SIZE
        head_stop = head_start + queries_per_group * HEAD_SIZE
        head_query = query_vectors[:, head_start:head_stop].reshape(
            row_count, queries_per_group, HEAD_SIZE
        )
        head_grad = cotangent[:, head_start:head_stop].reshape(
            row_count, queries_per_group, HEAD_SIZE
        )
        head_key = key_rows[:, shared_key_head * HEAD_SIZE : (shared_key_head + 1) * HEAD_SIZE]
        head_value = value_rows[:, shared_key_head * HEAD_SIZE : (shared_key_head + 1) * HEAD_SIZE]
        scores = (
            jnp.einsum("nhd,jd->nhj", head_query, head_key, preferred_element_type=jnp.float32)
            * score_scale
        )
        row_top = jnp.max(scores, axis=2, keepdims=True)
        exponent = jnp.exp(scores - row_top)
        row_total = jnp.sum(exponent, axis=2, keepdims=True)
        weights = exponent.astype(jnp.bfloat16)
        mixed_out = (
            jnp.einsum("nhj,jd->nhd", weights, head_value, preferred_element_type=jnp.float32)
            / row_total
        )
        inner_prod = jnp.sum(head_grad.astype(jnp.float32) * mixed_out, axis=2, keepdims=True)
        grad_prob = jnp.einsum(
            "nhd,jd->nhj", head_grad, head_value, preferred_element_type=jnp.float32
        )
        grad_score = (weights.astype(jnp.float32) / row_total * (grad_prob - inner_prod)).astype(
            jnp.bfloat16
        )
        query_gradient = (
            jnp.einsum("nhj,jd->nhd", grad_score, head_key, preferred_element_type=jnp.float32)
            * score_scale
        )
        pieces.append(query_gradient.reshape(row_count, queries_per_group * HEAD_SIZE))
    return jnp.concatenate(pieces, axis=1).astype(jnp.bfloat16)


def body(
    hidden,
    frozen_query_rows,
    output_gradient,
    token_log_ratio,
    lengths,
    response_win_probability,
    cached_prompt_keys,
    cached_prompt_values,
    adapter_down_factor,
    adapter_up_factor,
    attention_norm_gain,
):
    fsdp_count = lax.axis_size("fsdp")
    dp_index = lax.axis_index("dp")
    fsdp_index = lax.axis_index("fsdp")
    responses, per_device, single, feature_count = hidden.shape
    home_rows = responses * per_device
    local_rows = jnp.arange(per_device, dtype=jnp.int32)
    position = (dp_index * per_device + local_rows) * fsdp_count + fsdp_index
    is_valid = position[None, :] < lengths[:, None]
    partial_value = jnp.sum(jnp.where(is_valid, token_log_ratio[:, :, 0], 0.0), axis=1)
    seq_ratio = lax.psum(partial_value, ("dp", "fsdp"))
    weighting = 2.0 * (seq_ratio - target_scale * (response_win_probability - 0.5)) / responses
    down_full, up_full, gain_full = (
        lax.all_gather(adapter_down_factor, "fsdp", axis=0, tiled=True),
        lax.all_gather(adapter_up_factor, "fsdp", axis=1, tiled=True),
        lax.all_gather(attention_norm_gain, "fsdp", axis=0, tiled=True),
    )
    key_rows, value_rows = (
        lax.all_gather(cached_prompt_keys, "fsdp", axis=0, tiled=True),
        lax.all_gather(cached_prompt_values, "fsdp", axis=0, tiled=True),
    )
    widened = hidden.reshape(home_rows, feature_count).astype(jnp.float32)
    inverse = lax.rsqrt(jnp.mean(widened * widened, axis=1, keepdims=True) + norm_epsilon)
    normed_input = (widened * inverse * gain_full.astype(jnp.float32)).astype(jnp.bfloat16)
    lowrank_hidden = jnp.dot(normed_input, down_full, preferred_element_type=jnp.float32).astype(
        jnp.bfloat16
    )
    row_mask = is_valid.reshape(home_rows)
    row_coef = jnp.repeat(weighting, per_device)
    base_rows = frozen_query_rows.reshape(home_rows, -1)
    cotangent = jnp.where(
        row_mask[:, None],
        row_coef[:, None] * output_gradient.reshape(home_rows, -1).astype(jnp.float32),
        0.0,
    ).astype(jnp.bfloat16)
    query_vectors = (
        base_rows.astype(jnp.float32)
        + jnp.dot(lowrank_hidden, up_full, preferred_element_type=jnp.float32)
    ).astype(jnp.bfloat16)
    query_gradient = attend(query_vectors, cotangent, key_rows, value_rows)
    up_term = jnp.dot(lowrank_hidden.T, query_gradient, preferred_element_type=jnp.float32)
    gradient_lowrank = jnp.dot(
        query_gradient, up_full.T, preferred_element_type=jnp.float32
    ).astype(jnp.bfloat16)
    down_term = jnp.dot(normed_input.T, gradient_lowrank, preferred_element_type=jnp.float32)
    down_sum, up_sum = lax.psum((down_term, up_term), ("dp", "fsdp"))
    down_factor_part = adapter_down_factor.shape[0]
    up_factor_part = adapter_up_factor.shape[1]
    grad_down = lax.dynamic_slice_in_dim(
        down_sum, fsdp_index * down_factor_part, down_factor_part, 0
    )
    grad_up = lax.dynamic_slice_in_dim(up_sum, fsdp_index * up_factor_part, up_factor_part, 1)
    return (grad_down, grad_up, seq_ratio)


def solution(mesh):
    in_specs = (
        P(None, "dp", "fsdp", None),
        P(None, "dp", "fsdp", None),
        P(None, "dp", "fsdp", None),
        P(None, "dp", "fsdp"),
        P(),
        P(),
        P("fsdp", None),
        P("fsdp", None),
        P("fsdp", None),
        P(None, "fsdp"),
        P("fsdp"),
    )
    out_specs = (P("fsdp", None), P(None, "fsdp"), P())
    return jax.shard_map(body, mesh=mesh, in_specs=in_specs, out_specs=out_specs, check_vma=False)
```

profile of v0, /device:TPU:17, one launch (start us, length us, event | category | flops | bytes accessed | tf_op | source)
XLA Modules:
  0.0 574.0 jit_solution(2248930495816452318)
XLA Ops:
  9.6 105.0 %psum.21 = f32[4]{0:T(128)S(1)} all-reduce(f32[4]{0:T(128)S(1)} %get-tuple-element.5), channel_id=1, replica_groups=mesh['dp'=32,'fsdp'=16] {'dp','fsdp'}, use_global_device_ids=true, to_apply=%region_4.5 | all-reduce | flops 4 | bytes 32 | tf_op jit(solution)/shard_map/psum | solution.py:79
  116.1 2.1 multiply_reduce_fusion
  118.3 24.8 %all-gather = bf16[16,1,256]{2,1,0:T(2,128)(2,1)S(1)} all-gather(bf16[1,1,256]{2,1,0:T(2,128)(2,1)S(1)} %reshape.122), channel_id=1, replica_groups=mesh['dp'=32,'fsdp'=16] {'fsdp'}, dimensions={0}, use_global_device_ids=true | all-gather | bytes 8704 | tf_op jit(solution)/shard_map/all_gather | solution.py:84
  143.1 2.2 fusion.1
  152.9 24.4 %all_gather.17 = bf16[64,2048]{1,0:T(8,128)(2,1)S(1)} all-gather(bf16[64,128]{1,0:T(8,128)(2,1)S(1)} %copy-done.17), channel_id=1, replica_groups=mesh['dp'=32,'fsdp'=16] {'fsdp'}, dimensions={1}, use_global_device_ids=true | all-gather | bytes 278528 | tf_op jit(solution)/shard_map/all_gather | solution.py:83
  177.3 27.5 %all_gather.16 = bf16[4096,64]{0,1:T(8,128)(2,1)S(1)} all-gather(bf16[256,64]{0,1:T(8,128)(2,1)S(1)} %copy-done.16), channel_id=1, replica_groups=mesh['dp'=32,'fsdp'=16] {'fsdp'}, dimensions={0}, use_global_device_ids=true | all-gather | bytes 557056 | tf_op jit(solution)/shard_map/all_gather | solution.py:82
  208.8 2.0 copy-done
  211.9 3.0 fusion.39
  216.4 1.9 multiply_reduce_fusion.1
  218.3 1.9 copy-done.1
  222.0 3.1 fusion.30
  226.6 1.8 multiply_reduce_fusion.2
  228.4 2.0 copy-done.2
  232.1 3.1 fusion.33
  236.6 1.8 multiply_reduce_fusion.3
  238.4 1.9 copy-done.3
  242.3 3.1 fusion.36
  246.9 4.8 fusion.21
  251.7 4.8 fusion.24
  256.5 4.8 fusion.23
  261.3 4.8 fusion.22
  266.2 3.6 fusion.25
  269.8 2.2 fusion.70
  272.0 292.6 %all-reduce.3.cloned.1.call-done = (f32[4096,64]{0,1:T(8,128)}, f32[64,2048]{1,0:T(8,128)}) async-done(((f32[4096,64]{0,1:T(8,128)}, f32[64,2048]{1,0:T(8,128)}), (f32[4096,64]{0,1:T(8,128)}, f32[64,2048]{1,0:T(8,128)})) %all-reduce.3.cloned.1.call-update) | async-done | bytes 1572880 | tf_op jit(solution)/shard_map/psum | solution.py:114
  (106 shorter events, 30.8 us)
Async XLA Ops:
  7.2 138.2 %copy-start.6 = (bf16[4,64,1,2048]{3,1,2,0:T(8,128)(2,1)S(1)}, bf16[4,64,1,2048]{3,1,2,0:T(8,128)(2,1)}, u32[]{:S(2)}) copy-start(bf16[4,64,1,2048]{3,1,2,0:T(8,128)(2,1)} %param.13) | copy-start | bytes 3145732
  7.2 199.9 %all-gather.4.cloned.1.call-start = ((), (), s32[]{:S(2)}) async-start(), calls=%async_computation | async-start | bytes 1114112 | tf_op jit(solution)/shard_map/all_gather | solution.py:87
  7.9 204.0 %all-gather.6.cloned.1.call-start = ((), (), s32[]{:S(2)}) async-start(), calls=%async_computation.1 | async-start | bytes 1114112 | tf_op jit(solution)/shard_map/all_gather | solution.py:88
  8.7 555.9 %all-reduce.3.cloned.1.call-start = ((), (), s32[]{:S(2)}) async-start(), calls=%async_computation.2 | async-start | bytes 3145728 | tf_op jit(solution)/shard_map/psum | solution.py:114
  114.6 3.7 copy-start.31
  145.3 7.6 %copy-start.17 = (bf16[64,128]{1,0:T(8,128)(2,1)S(1)}, bf16[64,128]{1,0:T(8,128)(2,1)}, u32[]{:S(2)}) copy-start(bf16[64,128]{1,0:T(8,128)(2,1)} %param.20) | copy-start | bytes 49156
  145.4 32.0 %copy-start.16 = (bf16[256,64]{0,1:T(8,128)(2,1)S(1)}, bf16[256,64]{0,1:T(8,128)(2,1)}, u32[]{:S(2)}) copy-start(bf16[256,64]{0,1:T(8,128)(2,1)} %param.19) | copy-start | bytes 98308
  145.7 59.9 %copy-start.5 = (bf16[4,64,1,2048]{3,1,2,0:T(8,128)(2,1)S(1)}, bf16[4,64,1,2048]{3,1,2,0:T(8,128)(2,1)}, u32[]{:S(2)}) copy-start(bf16[4,64,1,2048]{3,1,2,0:T(8,128)(2,1)} %param.12) | copy-start | bytes 3145732
  210.8 4.2 copy-start.10
  211.7 6.6 %copy-start.18 = (f32[256,4]{0,1:T(4,128)}, f32[256,4]{0,1:T(4,128)S(1)}, u32[]{:S(2)}) copy-start(f32[256,4]{0,1:T(4,128)S(1)} %fusion.2) | copy-start | bytes 12292
  216.4 5.6 copy-start.4
  222.0 3.1 copy-start.11
  232.1 3.1 copy-start.12
  242.3 3.1 copy-start.13
  246.9 4.8 copy-start.20
  246.9 4.8 copy-start.25
  251.7 4.8 copy-start.22
  251.7 4.8 copy-start.26
  256.5 4.8 copy-start.24
  256.5 4.8 copy-start.27
  266.2 3.7 copy-start.15
  266.2 3.7 copy-start.28
  266.2 3.7 copy-start.29
  266.2 3.7 copy-start.30
  (11 other events, 20.1 us)
Sparse Core Ops, SparseCore 0:
  10.1 66.9 all-gather.3
  79.2 69.6 all-gather.5
  272.2 292.3 all-reduce.2
where the time goes:
time: 575 us; the launch traced here: 574 us
  waiting for transfers between devices  294 us (51%)
  blocking collectives  182 us (32%)
  matrix products  45.8 us (8%)
  local copies, waits for them, and re-layouts  25.3 us (4%)
  between operations  14.1 us (2%)
  other arithmetic  13.1 us (2%)
    psum x1, waiting for transfers between devices, body(): down_sum, up_sum = lax.psum((down_term, up_term), ('dp', 'fsdp'))  293 us
    psum x1, blocking collectives, body(): seq_ratio = lax.psum(partial_value, ('dp', 'fsdp'))  105 us
    all_gather x1, blocking collectives, body(): lax.all_gather(adapter_down_factor, 'fsdp', axis=0, tiled=True)  27.5 us
    all_gather x1, blocking collectives, body(): lax.all_gather(attention_norm_gain, 'fsdp', axis=0, tiled=True)  24.8 us
    all_gather x1, blocking collectives, body(): lax.all_gather(adapter_up_factor, 'fsdp', axis=1, tiled=True)  24.4 us
    dot_general x4, matrix products, attend(): jnp.einsum('nhj,jd->nhd', grad_score, head_key, preferred_element_type=jn...  19.2 us
    dot_general x4, matrix products, attend(): jnp.einsum('nhj,jd->nhd', weights, head_value, preferred_element_type=jnp...  12.3 us
  transfers between devices with their start and end apart: 3, of which 1 were waited for; matrix products, arithmetic and copies ran while one was open for 3% of the time, Pallas kernels for 0%

commit v1 on v0

--- a/solution.py
+++ b/solution.py
@@ -111,7 +111,7 @@
         query_gradient, up_full.T, preferred_element_type=jnp.float32
     ).astype(jnp.bfloat16)
     down_term = jnp.dot(normed_input.T, gradient_lowrank, preferred_element_type=jnp.float32)
-    down_sum, up_sum = lax.psum((down_term, up_term), ("dp", "fsdp"))
+    down_sum, up_sum = lax.psum(lax.psum((down_term, up_term), "fsdp"), "dp")
     down_factor_part = adapter_down_factor.shape[0]
     up_factor_part = adapter_up_factor.shape[1]
     grad_down = lax.dynamic_slice_in_dim(

time: 575 us -> 737 us (1.28)
  the two profiles are of different devices: /device:TPU:17 before, /device:TPU:1 now
where the time goes in v1:
time: 737 us; the launch traced here: 736 us
  waiting for transfers between devices  454 us (62%)
  blocking collectives  183 us (25%)
  matrix products  45.8 us (6%)
  local copies, waits for them, and re-layouts  25.2 us (3%)
  between operations  14.1 us (2%)
  other arithmetic  13.1 us (2%)
    psum x2, waiting for transfers between devices, body(): down_sum, up_sum = lax.psum(lax.psum((down_term, up_term), 'fsdp'), 'dp')  453 us
    psum x1, blocking collectives, body(): seq_ratio = lax.psum(partial_value, ('dp', 'fsdp'))  107 us
    all_gather x1, blocking collectives, body(): lax.all_gather(adapter_down_factor, 'fsdp', axis=0, tiled=True)  27.2 us
    all_gather x1, blocking collectives, body(): lax.all_gather(attention_norm_gain, 'fsdp', axis=0, tiled=True)  24.9 us
    all_gather x1, blocking collectives, body(): lax.all_gather(adapter_up_factor, 'fsdp', axis=1, tiled=True)  24 us
    dot_general x4, matrix products, attend(): jnp.einsum('nhj,jd->nhd', grad_score, head_key, preferred_element_type=jn...  19.2 us
  transfers between devices with their start and end apart: 4, of which 2 were waited for; matrix products, arithmetic and copies ran while one was open for 3% of the time, Pallas kernels for 0%

profile of v1, /device:TPU:1, one launch (start us, length us, event | category | flops | bytes accessed | tf_op | source)
XLA Modules:
  0.0 736.0 jit_solution(5776984234282004746)
XLA Ops:
  9.6 107.1 %psum.35 = f32[4]{0:T(128)S(1)} all-reduce(f32[4]{0:T(128)S(1)} %get-tuple-element.7), channel_id=1, replica_groups=mesh['dp'=32,'fsdp'=16] {'dp','fsdp'}, use_global_device_ids=true, to_apply=%region_4.5 | all-reduce | flops 4 | bytes 32 | tf_op jit(solution)/shard_map/psum | solution.py:79
  118.3 2.1 multiply_reduce_fusion
  120.5 24.9 %all-gather = bf16[16,1,256]{2,1,0:T(2,128)(2,1)S(1)} all-gather(bf16[1,1,256]{2,1,0:T(2,128)(2,1)S(1)} %reshape.122), channel_id=1, replica_groups=mesh['dp'=32,'fsdp'=16] {'fsdp'}, dimensions={0}, use_global_device_ids=true | all-gather | bytes 8704 | tf_op jit(solution)/shard_map/all_gather | solution.py:84
  145.4 2.2 fusion.1
  155.2 24.0 %all_gather.17 = bf16[64,2048]{1,0:T(8,128)(2,1)S(1)} all-gather(bf16[64,128]{1,0:T(8,128)(2,1)S(1)} %copy-done.17), channel_id=1, replica_groups=mesh['dp'=32,'fsdp'=16] {'fsdp'}, dimensions={1}, use_global_device_ids=true | all-gather | bytes 278528 | tf_op jit(solution)/shard_map/all_gather | solution.py:83
  179.2 27.2 %all_gather.16 = bf16[4096,64]{0,1:T(8,128)(2,1)S(1)} all-gather(bf16[256,64]{0,1:T(8,128)(2,1)S(1)} %copy-done.16), channel_id=1, replica_groups=mesh['dp'=32,'fsdp'=16] {'fsdp'}, dimensions={0}, use_global_device_ids=true | all-gather | bytes 557056 | tf_op jit(solution)/shard_map/all_gather | solution.py:82
  210.5 2.0 copy-done
  213.6 3.0 fusion.39
  218.1 1.9 multiply_reduce_fusion.1
  220.0 1.9 copy-done.1
  223.7 3.1 fusion.30
  230.0 1.9 copy-done.2
  233.7 3.1 fusion.33
  238.2 1.8 multiply_reduce_fusion.3
  240.1 1.9 copy-done.3
  243.9 3.1 fusion.36
  248.5 4.8 fusion.21
  253.3 4.8 fusion.24
  258.2 4.8 fusion.23
  263.0 4.8 fusion.22
  267.8 3.6 fusion.25
  271.4 2.2 fusion.70
  273.7 149.1 %all-reduce.7.cloned.1.call-done = (f32[4096,64]{0,1:T(8,128)}, f32[64,2048]{1,0:T(8,128)}) async-done(((f32[4096,64]{0,1:T(8,128)}, f32[64,2048]{1,0:T(8,128)}), (f32[4096,64]{0,1:T(8,128)}, f32[64,2048]{1,0:T(8,128)})) %all-reduce.7.cloned.1.call-update) | async-done | bytes 1572880 | tf_op jit(solution)/shard_map/psum | solution.py:114
  422.9 303.7 %all-reduce.5.cloned.1.call-done = (f32[4096,64]{0,1:T(8,128)}, f32[64,2048]{1,0:T(8,128)}) async-done(((f32[4096,64]{0,1:T(8,128)}, f32[64,2048]{1,0:T(8,128)}), (f32[4096,64]{0,1:T(8,128)}, f32[64,2048]{1,0:T(8,128)})) %all-reduce.5.cloned.1.call-update) | async-done | bytes 1572880 | tf_op jit(solution)/shard_map/psum | solution.py:114
  (109 shorter events, 32.7 us)
Async XLA Ops:
  7.2 140.4 %copy-start.6 = (bf16[4,64,1,2048]{3,1,2,0:T(8,128)(2,1)S(1)}, bf16[4,64,1,2048]{3,1,2,0:T(8,128)(2,1)}, u32[]{:S(2)}) copy-start(bf16[4,64,1,2048]{3,1,2,0:T(8,128)(2,1)} %param.13) | copy-start | bytes 3145732
  7.2 201.6 %all-gather.4.cloned.1.call-start = ((), (), s32[]{:S(2)}) async-start(), calls=%async_computation | async-start | bytes 1114112 | tf_op jit(solution)/shard_map/all_gather | solution.py:87
  7.9 205.7 %all-gather.6.cloned.1.call-start = ((), (), s32[]{:S(2)}) async-start(), calls=%async_computation.1 | async-start | bytes 1114112 | tf_op jit(solution)/shard_map/all_gather | solution.py:88
  8.7 414.2 %all-reduce.7.cloned.1.call-start = ((), (), s32[]{:S(2)}) async-start(), calls=%async_computation.3 | async-start | bytes 3145728 | tf_op jit(solution)/shard_map/psum | solution.py:114
  116.7 3.7 copy-start.31
  147.6 7.6 %copy-start.17 = (bf16[64,128]{1,0:T(8,128)(2,1)S(1)}, bf16[64,128]{1,0:T(8,128)(2,1)}, u32[]{:S(2)}) copy-start(bf16[64,128]{1,0:T(8,128)(2,1)} %param.20) | copy-start | bytes 49156
  147.6 31.6 %copy-start.16 = (bf16[256,64]{0,1:T(8,128)(2,1)S(1)}, bf16[256,64]{0,1:T(8,128)(2,1)}, u32[]{:S(2)}) copy-start(bf16[256,64]{0,1:T(8,128)(2,1)} %param.19) | copy-start | bytes 98308
  148.0 59.2 %copy-start.5 = (bf16[4,64,1,2048]{3,1,2,0:T(8,128)(2,1)S(1)}, bf16[4,64,1,2048]{3,1,2,0:T(8,128)(2,1)}, u32[]{:S(2)}) copy-start(bf16[4,64,1,2048]{3,1,2,0:T(8,128)(2,1)} %param.12) | copy-start | bytes 3145732
  212.5 4.2 copy-start.10
  213.4 6.6 copy-start.18
  218.1 5.6 copy-start.4
  223.7 3.1 copy-start.11
  243.9 3.1 copy-start.13
  248.5 4.8 copy-start.20
  248.5 4.8 copy-start.25
  253.3 4.8 copy-start.22
  253.3 4.8 copy-start.26
  258.1 4.8 copy-start.24
  258.1 4.8 copy-start.27
  267.8 3.7 copy-start.15
  267.8 3.7 copy-start.28
  267.8 3.7 copy-start.29
  267.8 3.7 copy-start.30
  273.7 453.0 %all-reduce.5.cloned.1.call-start = ((), (), s32[]{:S(2)}) async-start(), calls=%async_computation.2 | async-start | bytes 3145728 | tf_op jit(solution)/shard_map/psum | solution.py:114
  (12 other events, 23.2 us)
Sparse Core Ops, SparseCore 0:
  10.1 67.9 all-gather.3
  80.1 70.1 all-gather.5
  273.8 149.0 all-reduce.6
  426.0 300.6 all-reduce.4
